TPU v7x, 32 devices: a whole 2x2x4 slice. The times are simulated.
32 devices in a mesh: rep: 2 (over y), head: 4 (over z), ctx: 4 (over x, core).
Axes of the slice: x: 2, y: 2, z: 4, core: 2. Of those that a mesh axis runs over, the one named last changes fastest.
Arguments:
- queries: bfloat16 [8, 512, 8192], P(('rep', 'ctx'), 'head'), parts along dimension 0, may hold values from -6 to 6
- keys: bfloat16 [8, 512, 8192], P(('rep', 'ctx'), 'head'), parts along dimension 0, may hold values from -6 to 6
- values: bfloat16 [8, 512, 8192], P(('rep', 'ctx'), 'head'), parts along dimension 0, may hold values from -6 to 6
- gain: float32 [8192], replicated, may hold values from 0.5 to 1.5
Outputs:
- normed: bfloat16 [8, 512, 8192], P(('rep', 'ctx'), 'head'), parts along dimension 0
There are 2 independent parts, one for each index of `rep`. A program takes and returns all parts, laid end to end along the dimension named above; an argument that names none is the same for every part. Nothing has to cross between parts.
All inputs are finite; a program needn't handle non-finite values.
Results may differ from a plain program's by a relative error of at most 0.0059.
Values may be sent and summed in bfloat16 or wider, within the bound.
No kernel may reach another device: no remote copies, remote signals or barrier semaphores. Data moves between devices by JAX's collectives and lax.ppermute only.
A program may use at most 128 MiB of HBM per device.

v0:
```python
import jax
import jax.numpy as jnp
from jax import lax
from jax.sharding import PartitionSpec as P

DH = 128


def entering(part, axis, combine, identity):
    place = lax.axis_index(axis)
    gathered = lax.all_gather(part, axis)
    state = jnp.zeros_like(part) + jnp.asarray(identity, part.dtype)

    def one(step, state):
        return combine(state, lax.dynamic_index_in_dim(gathered, step, 0, False))

    return lax.fori_loop(0, place, one, state)


def block_attention(query_blk, key_blk, value_blk, state_blk):
    length = query_blk.shape[-2]
    causal = jnp.arange(length)[:, None] >= jnp.arange(length)[None, :]
    scores = jnp.einsum(
        "...htd,...hsd->...hts", query_blk, key_blk, preferred_element_type=jnp.float32
    )
    scores = jnp.where(causal, scores, jnp.float32(0.0)).astype(jnp.bfloat16)
    local_part = jnp.einsum(
        "...hts,...hsd->...htd", scores, value_blk, preferred_element_type=jnp.float32
    )
    carried = jnp.einsum(
        "...htd,...hde->...hte", query_blk, state_blk, preferred_element_type=jnp.float32
    )
    return (local_part + carried).astype(jnp.bfloat16)


def activate(rows):
    return jax.nn.silu(rows.astype(jnp.float32)).astype(jnp.bfloat16)


def row_norm(attn, gain):
    wide = attn.astype(jnp.float32)
    mean_sq = jnp.mean(wide * wide, axis=1, keepdims=True)
    return (wide * lax.rsqrt(mean_sq + 1e-06) * gain[None, :]).astype(jnp.bfloat16)


def body(queries, keys, values, gain):
    tok_rows = queries.shape[1]
    width = queries.shape[2]
    q_rows = queries.reshape(tok_rows, width)
    k_rows = keys.reshape(tok_rows, width)
    v_rows = values.reshape(tok_rows, width)
    head_q, head_k, head_v = (
        lax.all_to_all(q_rows, "head", split_axis=1, concat_axis=0, tiled=True),
        lax.all_to_all(k_rows, "head", split_axis=1, concat_axis=0, tiled=True),
        lax.all_to_all(v_rows, "head", split_axis=1, concat_axis=0, tiled=True),
    )
    span = head_q.shape[0]
    local_cols = head_q.shape[1]
    local_heads = local_cols // DH
    blocks = span // tok_rows
    query_hb = activate(head_q).reshape(blocks, tok_rows, local_heads, DH).transpose(0, 2, 1, 3)
    key_hb = activate(head_k).reshape(blocks, tok_rows, local_heads, DH).transpose(0, 2, 1, 3)
    value_hb = head_v.reshape(blocks, tok_rows, local_heads, DH).transpose(0, 2, 1, 3)
    block_states = jnp.einsum(
        "bhtd,bhte->bhde", key_hb, value_hb, preferred_element_type=jnp.float32
    )
    stretch_total = jnp.sum(block_states, axis=0)
    earlier = entering(
        stretch_total, "ctx", lambda first, second: first + second, jnp.zeros_like(stretch_total)
    )
    running = jnp.cumsum(block_states, axis=0)
    within = jnp.concatenate([jnp.zeros_like(running[:1]), running[:-1]], axis=0)
    states = (earlier[None] + within).astype(jnp.bfloat16)
    attn = block_attention(query_hb, key_hb, value_hb, states)
    attn = attn.transpose(0, 2, 1, 3).reshape(span, local_cols)
    back = lax.all_to_all(attn, "head", split_axis=0, concat_axis=1, tiled=True)
    normed = row_norm(back, gain)
    return normed.reshape(1, tok_rows, width)


def solution(mesh):
    return jax.shard_map(
        body,
        mesh=mesh,
        in_specs=(
            P(("rep", "ctx"), "head", None),
            P(("rep", "ctx"), "head", None),
            P(("rep", "ctx"), "head", None),
            P(),
        ),
        out_specs=P(("rep", "ctx"), "head", None),
        check_vma=False,
    )
```

profile of v0, /device:TPU:2, one launch (start us, length us, event | category | flops | bytes accessed | tf_op | source)
XLA Modules:
  0.0 270.1 jit_solution(5377043979471332079)
XLA Ops:
  6.5 4.1 %copy.18 = bf16[1,128,8192]{1,2,0:T(8,128)(2,1)} copy(bf16[1,128,8192]{2,1,0:T(8,128)(2,1)} %param.7) | data formatting | bytes 4194304 | tf_op args[1]
  10.6 4.9 %all-to-all-start.1 = ((bf16[128,4,2048]{0,2,1:T(8,128)(2,1)}), bf16[128,4,2048]{0,2,1:T(8,128)(2,1)S(1)}, u32[]{:S(2)}, u32[]{:S(2)}) async-start(bf16[128,4,2048]{0,2,1:T(8,128)(2,1)} %bitcast.47), calls=%async_computation.1 | async-start | bytes 4194304 | tf_op jit(solution)/shard_map/all_to_all | solution.py:54
  15.5 4.1 %copy.31 = bf16[1,128,8192]{1,2,0:T(8,128)(2,1)} copy(bf16[1,128,8192]{2,1,0:T(8,128)(2,1)} %param.8) | data formatting | bytes 4194304 | tf_op jit(solution)/shard_map/all_to_all | solution.py:55
  19.5 44.1 %all-to-all-done.1 = bf16[128,4,2048]{0,2,1:T(8,128)(2,1)S(1)} async-done(((bf16[128,4,2048]{0,2,1:T(8,128)(2,1)}), bf16[128,4,2048]{0,2,1:T(8,128)(2,1)S(1)}, u32[]{:S(2)}, u32[]{:S(2)}) %all-to-all-start.1) | async-done | bytes 2097184 | tf_op jit(solution)/shard_map/all_to_all | solution.py:54
  63.7 4.4 %all-to-all-start.2 = ((bf16[128,4,2048]{0,2,1:T(8,128)(2,1)}), bf16[128,4,2048]{0,2,1:T(8,128)(2,1)}, u32[]{:S(2)}, u32[]{:S(2)}) async-start(bf16[128,4,2048]{0,2,1:T(8,128)(2,1)} %bitcast.46), calls=%async_computation.2 | async-start | bytes 4194304 | tf_op jit(solution)/shard_map/all_to_all | solution.py:55
  68.1 2.2 convert_element_type.92
  70.4 45.5 %all-to-all-done.2 = bf16[128,4,2048]{0,2,1:T(8,128)(2,1)} async-done(((bf16[128,4,2048]{0,2,1:T(8,128)(2,1)}), bf16[128,4,2048]{0,2,1:T(8,128)(2,1)}, u32[]{:S(2)}, u32[]{:S(2)}) %all-to-all-start.2) | async-done | bytes 2097184 | tf_op jit(solution)/shard_map/all_to_all | solution.py:55
  115.9 7.3 %fusion.13 = (f32[16,128,128]{2,1,0:T(8,128)}, f32[4,16,128,128]{3,2,1,0:T(8,128)}) fusion(bf16[4,16,128,128]{2,3,1,0:T(8,128)(2,1)} %bitcast.14, f32[4,128,16,128]{1,3,2,0:T(8,128)} %bitcast.51), kind=kOutput, calls=%fused_computation.19 | convolution fusion | flops 274464768 | bytes 11534336 | tf_op jit(solution)/shard_map/bhtd,bhte->bhde/dot_general | solution.py:64
  123.2 2.4 copy.17
  125.7 3.6 %all-to-all-start = ((bf16[128,4,2048]{0,2,1:T(8,128)(2,1)}), bf16[128,4,2048]{0,2,1:T(8,128)(2,1)S(1)}, u32[]{:S(2)}, u32[]{:S(2)}) async-start(bf16[128,4,2048]{0,2,1:T(8,128)(2,1)} %bitcast.45), calls=%async_computation | async-start | bytes 4194304 | tf_op jit(solution)/shard_map/all_to_all | solution.py:53
  129.3 3.1 %fusion.14 = f32[4,16,128,128]{3,2,1,0:T(8,128)S(1)} fusion(f32[4,16,128,128]{3,2,1,0:T(8,128)} %get-tuple-element.38), kind=kOutput, calls=%fused_computation.20 | output fusion | flops 3145728 | bytes 8388608 | tf_op jit(solution)/shard_map/jit(cumsum)/reduce_window_sum | solution.py:71
  132.5 2.0 slice.4
  134.5 42.5 %all-to-all-done = bf16[128,4,2048]{0,2,1:T(8,128)(2,1)S(1)} async-done(((bf16[128,4,2048]{0,2,1:T(8,128)(2,1)}), bf16[128,4,2048]{0,2,1:T(8,128)(2,1)S(1)}, u32[]{:S(2)}, u32[]{:S(2)}) %all-to-all-start) | async-done | bytes 2097184 | tf_op jit(solution)/shard_map/all_to_all | solution.py:53
  176.9 2.2 convert_element_type.91
  179.2 10.1 %fusion.8 = f32[4,16,128,128]{2,3,1,0:T(8,128)} fusion(bf16[4,16,128,128]{2,3,1,0:T(8,128)(2,1)} %bitcast.14, pred[128,128]{1,0:T(8,128)(4,1)S(1)} %iota_compare_fusion, f32[4,128,16,128]{1,3,2,0:T(8,128)} %bitcast.49, f32[4,128,16,128]{1,3,2,0:T(8,128)} %bitcast.52), kind=kOutput, calls=%fused_computation.14 | convolution fusion | flops 549453824 | bytes 14696448 | tf_op jit(solution)/shard_map/...hts,...hsd->...htd/dot_general | solution.py:27
  189.4 3.0 %while.10 = (s32[]{:T(128)}, f32[16,128,128]{2,1,0:T(8,128)S(1)}, s32[]{:T(128)}, f32[4,16,128,128]{3,2,1,0:T(8,128)}, s32[]{:T(128)}, /*index=5*/s32[]{:T(128)}, s32[]{:T(128)}) while((s32[]{:T(128)}, f32[16,128,128]{2,1,0:T(8,128)S(1)}, s32[]{:T(128)}, f32[4,16,128,128]{3,2,1,0:T(8,128)}, s32[]{:T(128)}, /*index=5*/s32[]{:T(128)}, ...), condition=%wide.region_2.3_spmd, body=%wide.region_1.2_spmd.sunk | while | flops 262149 | bytes 3145843 | solution.py:17
  189.4 1.5 bitcast_add_fusion.2
  190.9 1.5 bitcast_add_fusion.2
  192.4 6.2 %add_convert_fusion = bf16[4,16,128,128]{2,3,1,0:T(8,128)(2,1)S(1)} fusion(f32[4,16,128,128]{2,3,1,0:T(8,128)} %fusion.8, f32[3,16,128,128]{3,2,1,0:T(8,128)} %slice.4, f32[16,128,128]{2,1,0:T(8,128)S(1)} %get-tuple-element.28, f32[4,128,16,128]{1,3,2,0:T(8,128)} %bitcast.50), kind=kOutput, calls=%fused_computation.3 | convolution fusion | flops 277872640 | bytes 14680064 | tf_op jit(solution)/shard_map/...htd,...hde->...hte/dot_general | solution.py:30
  198.6 51.7 %all_to_all.55 = bf16[4,128,2048]{1,2,0:T(8,128)(2,1)S(1)} all-to-all(bf16[4,128,2048]{1,2,0:T(8,128)(2,1)S(1)} %bitcast.53), channel_id=1, replica_groups=mesh['rep'=2,'head'=4,'ctx'=4] {'head'}, dimensions={0} | all-to-all | bytes 4194304 | tf_op jit(solution)/shard_map/all_to_all | solution.py:76
  250.3 2.2 convert_element_type.93
  252.5 5.6 %copy.32 = f32[1,128,8192]{2,1,0:T(8,128)} copy(f32[1,128,8192]{1,2,0:T(8,128)} %bitcast.44) | data formatting | bytes 8388608 | tf_op jit(solution)/shard_map/convert_element_type | solution.py:41
  258.1 1.1 multiply_reduce_fusion
  259.2 4.0 %multiply_convert_fusion = bf16[1,128,8192]{2,1,0:T(8,128)(2,1)} fusion(f32[1,128,8192]{2,1,0:T(8,128)} %copy.32, f32[8192]{0:T(1024)S(1)} %copy-done.1, f32[128]{0:T(128)S(1)} %add_rsqrt_fusion), kind=kLoop, calls=%fused_computation.1 | loop fusion | flops 3145728 | bytes 6324736 | tf_op jit(solution)/shard_map/convert_element_type | solution.py:43
  (10 shorter events, 0.2 us)
Async XLA Ops:
  10.6 53.1 %all-to-all-start.1 = ((bf16[128,4,2048]{0,2,1:T(8,128)(2,1)}), bf16[128,4,2048]{0,2,1:T(8,128)(2,1)S(1)}, u32[]{:S(2)}, u32[]{:S(2)}) async-start(bf16[128,4,2048]{0,2,1:T(8,128)(2,1)} %bitcast.47), calls=%async_computation.1 | async-start | bytes 4194304 | tf_op jit(solution)/shard_map/all_to_all | solution.py:54
  63.7 52.2 %all-to-all-start.2 = ((bf16[128,4,2048]{0,2,1:T(8,128)(2,1)}), bf16[128,4,2048]{0,2,1:T(8,128)(2,1)}, u32[]{:S(2)}, u32[]{:S(2)}) async-start(bf16[128,4,2048]{0,2,1:T(8,128)(2,1)} %bitcast.46), calls=%async_computation.2 | async-start | bytes 4194304 | tf_op jit(solution)/shard_map/all_to_all | solution.py:55
  68.1 121.2 %all-gather.3.cloned.1.call-start = ((), (), s32[]{:S(2)}) async-start(), calls=%async_computation.4 | async-start | bytes 5242880 | tf_op jit(solution)/shard_map/all_gather | solution.py:11
  115.9 7.3 %copy-start = (bf16[1,128,8192]{2,1,0:T(8,128)(2,1)S(1)}, bf16[1,128,8192]{2,1,0:T(8,128)(2,1)}, u32[]{:S(2)}) copy-start(bf16[1,128,8192]{2,1,0:T(8,128)(2,1)} %param.6) | copy-start | bytes 6291460
  125.7 51.3 %all-to-all-start = ((bf16[128,4,2048]{0,2,1:T(8,128)(2,1)}), bf16[128,4,2048]{0,2,1:T(8,128)(2,1)S(1)}, u32[]{:S(2)}, u32[]{:S(2)}) async-start(bf16[128,4,2048]{0,2,1:T(8,128)(2,1)} %bitcast.45), calls=%async_computation | async-start | bytes 4194304 | tf_op jit(solution)/shard_map/all_to_all | solution.py:53
  252.5 6.7 %copy-start.1 = (f32[8192]{0:T(1024)S(1)}, f32[8192]{0:T(1024)}, u32[]{:S(2)}) copy-start(f32[8192]{0:T(1024)} %param.9) | copy-start | bytes 98308
Sparse Core Ops, SparseCore 0:
  123.3 32.4 all-gather.2
where the time goes:
time: 271 us; the launch traced here: 270 us
  waiting for transfers between devices  132 us (49%)
  blocking collectives  51.7 us (19%)
  matrix products  23.6 us (9%)
  local copies, waits for them, and re-layouts  18.3 us (7%)
  other arithmetic  17.9 us (7%)
  between operations  13.5 us (5%)
  starting transfers between devices  13 us (5%)
    all_to_all x1, blocking collectives, body(): back = lax.all_to_all(attn, 'head', split_axis=0, concat_axis=1, tiled=True)  51.7 us
    all_to_all x1, waiting for transfers between devices, body(): lax.all_to_all(v_rows, 'head', split_axis=1, concat_axis=0, tiled=True)  45.5 us
    all_to_all x1, waiting for transfers between devices, body(): lax.all_to_all(k_rows, 'head', split_axis=1, concat_axis=0, tiled=True)  44.1 us
    all_to_all x1, waiting for transfers between devices, body(): lax.all_to_all(q_rows, 'head', split_axis=1, concat_axis=0, tiled=True)  42.5 us
    dot_general x1, matrix products, block_attention(): jnp.einsum('...hts,...hsd->...htd', scores, value_blk, preferred_element_...  10.1 us
    dot_general x1, matrix products, body(): jnp.einsum('bhtd,bhte->bhde', key_hb, value_hb, preferred_element_type=jn...  7.32 us
    unnamed x6, local copies, waits for them, and re-layouts  6.5 us
    dot_general x1, matrix products, block_attention(): jnp.einsum('...htd,...hde->...hte', query_blk, state_blk, preferred_eleme...  6.17 us
  transfers between devices with their start and end apart: 4, of which 3 were waited for; matrix products, arithmetic and copies ran while one was open for 10% of the time, Pallas kernels for 0%

commit v1 on v0

--- a/solution.py
+++ b/solution.py
@@ -4,6 +4,18 @@
 from jax.sharding import PartitionSpec as P
 
 DH = 128
+
+
+def sent_to_each(x, axis, split, join):
+    ways, here = (lax.axis_size(axis), lax.axis_index(axis))
+    width = x.shape[split] // ways
+    turned = jnp.roll(x, -here * width, axis=split)
+    got = [lax.slice_in_dim(turned, 0, width, axis=split)]
+    for far in range(1, ways):
+        sent = lax.slice_in_dim(turned, far * width, (far + 1) * width, axis=split)
+        got.append(lax.ppermute(sent, axis, [(d, (d + far) % ways) for d in range(ways)]))
+    line = jnp.concatenate(got[::-1], axis=join)
+    return jnp.roll(line, (here + 1) * got[0].shape[join], axis=join)
 
 
 def entering(part, axis, combine, identity):
@@ -73,7 +85,7 @@
     states = (earlier[None] + within).astype(jnp.bfloat16)
     attn = block_attention(query_hb, key_hb, value_hb, states)
     attn = attn.transpose(0, 2, 1, 3).reshape(span, local_cols)
-    back = lax.all_to_all(attn, "head", split_axis=0, concat_axis=1, tiled=True)
+    back = sent_to_each(attn, "head", 0, 1)
     normed = row_norm(back, gain)
     return normed.reshape(1, tok_rows, width)
 

time: 271 us -> 263 us (0.970)
  blocking collectives: 51.7 us -> 0 us
  waiting for transfers between devices: 132 us -> 174 us
  local copies, waits for them, and re-layouts: 18.3 us -> 25.5 us
  other arithmetic: 17.9 us -> 13.2 us
  matrix products: 23.6 us -> 19.6 us
    all_to_all x1 -> x0, blocking collectives: 51.7 us -> none  [body(): back = lax.all_to_all(attn, 'head', split_axis=0, concat_axis=1, tiled=True)]
    ppermute x0 -> x3, waiting for transfers between devices: none -> 44.1 us  [sent_to_each(): lax.ppermute(sent, axis, [(d, (d + far) % ways) for d in range(ways)])]
    unnamed x6 -> x21, local copies, waits for them, and re-layouts: 6.5 us -> 16.9 us
    convert_element_type x2 -> x0, other arithmetic: 6.22 us -> none  [the longest x1 4.01 us: row_norm(): (wide * lax.rsqrt(mean_sq + 1e-06) * gain[None, :]).astype(jnp.bfloat16)]
    convert_element_type x1, local copies, waits for them, and re-layouts: 5.6 us -> 1.36 us  [block_attention(): return (local_part + carried).astype(jnp.bfloat16)]
    all_to_all x1 -> x0, local copies, waits for them, and re-layouts: 4.06 us -> none  [body(): lax.all_to_all(v_rows, 'head', split_axis=1, concat_axis=0, tiled=True)]
    reshape x0 -> x1, local copies, waits for them, and re-layouts: none -> 3.95 us  [body(): head_v.reshape(blocks, tok_rows, local_heads, DH).transpose(0, 2, 1, 3)]
    dot_general x1, matrix products: 7.32 us -> 4.37 us  [body(): jnp.einsum('bhtd,bhte->bhde', key_hb, value_hb, preferred_element_type=jn...]
  transfers between devices with their start and end apart: 4 -> 7, of which waited for: 3 -> 5; matrix products, arithmetic and copies ran while one was open for 10% -> 10% of each run, Pallas kernels for 0% -> 0%
where the time goes in v1:
time: 263 us; the launch traced here: 261 us
  waiting for transfers between devices  174 us (66%)
  local copies, waits for them, and re-layouts  25.5 us (10%)
  matrix products  19.6 us (7%)
  starting transfers between devices  14.2 us (5%)
  between operations  13.6 us (5%)
  other arithmetic  13.2 us (5%)
    ppermute x3, waiting for transfers between devices, sent_to_each(): lax.ppermute(sent, axis, [(d, (d + far) % ways) for d in range(ways)])  44.1 us
    all_to_all x1, waiting for transfers between devices, body(): lax.all_to_all(v_rows, 'head', split_axis=1, concat_axis=0, tiled=True)  44.1 us
    all_to_all x1, waiting for transfers between devices, body(): lax.all_to_all(k_rows, 'head', split_axis=1, concat_axis=0, tiled=True)  43.7 us
    all_to_all x1, waiting for transfers between devices, body(): lax.all_to_all(q_rows, 'head', split_axis=1, concat_axis=0, tiled=True)  42.5 us
    unnamed x21, local copies, waits for them, and re-layouts  16.9 us
    dot_general x1, matrix products, block_attention(): jnp.einsum('...hts,...hsd->...htd', scores, value_blk, preferred_element_...  9.27 us
    dot_general x1, matrix products, block_attention(): jnp.einsum('...htd,...hde->...hte', query_blk, state_blk, preferred_eleme...  5.94 us
  transfers between devices with their start and end apart: 7, of which 5 were waited for; matrix products, arithmetic and copies ran while one was open for 10% of the time, Pallas kernels for 0%

profile of v1, /device:TPU:2, one launch (start us, length us, event | category | flops | bytes accessed | tf_op | source)
XLA Modules:
  0.0 260.7 jit_solution(6231302050535737118)
XLA Ops:
  6.5 4.1 %copy.16 = bf16[1,128,8192]{1,2,0:T(8,128)(2,1)} copy(bf16[1,128,8192]{2,1,0:T(8,128)(2,1)} %param.8) | data formatting | bytes 4194304 | tf_op args[2]
  10.6 4.9 %all-to-all-start.2 = ((bf16[128,4,2048]{0,2,1:T(8,128)(2,1)}), bf16[128,4,2048]{0,2,1:T(8,128)(2,1)S(1)}, u32[]{:S(2)}, u32[]{:S(2)}) async-start(bf16[128,4,2048]{0,2,1:T(8,128)(2,1)} %bitcast.55), calls=%async_computation.2 | async-start | bytes 4194304 | tf_op jit(solution)/shard_map/all_to_all | solution.py:67
  15.5 4.1 %copy.13 = bf16[1,128,8192]{1,2,0:T(8,128)(2,1)} copy(bf16[1,128,8192]{2,1,0:T(8,128)(2,1)} %param.7) | data formatting | bytes 4194304 | tf_op args[1]
  19.5 44.1 %all-to-all-done.2 = bf16[128,4,2048]{0,2,1:T(8,128)(2,1)S(1)} async-done(((bf16[128,4,2048]{0,2,1:T(8,128)(2,1)}), bf16[128,4,2048]{0,2,1:T(8,128)(2,1)S(1)}, u32[]{:S(2)}, u32[]{:S(2)}) %all-to-all-start.2) | async-done | bytes 2097184 | tf_op jit(solution)/shard_map/all_to_all | solution.py:67
  65.0 3.6 %all-to-all-start.1 = ((bf16[128,4,2048]{0,2,1:T(8,128)(2,1)}), bf16[128,4,2048]{0,2,1:T(8,128)(2,1)S(1)}, u32[]{:S(2)}, u32[]{:S(2)}) async-start(bf16[128,4,2048]{0,2,1:T(8,128)(2,1)} %bitcast.54), calls=%async_computation.1 | async-start | bytes 4194304 | tf_op jit(solution)/shard_map/all_to_all | solution.py:66
  68.6 3.9 %copy.17 = bf16[4,128,16,128]{3,1,2,0:T(8,128)(2,1)} copy(bf16[4,128,16,128]{1,3,2,0:T(8,128)(2,1)} %bitcast.53) | data formatting | bytes 4194304 | tf_op jit(solution)/shard_map/reshape | solution.py:75
  72.6 43.7 %all-to-all-done.1 = bf16[128,4,2048]{0,2,1:T(8,128)(2,1)S(1)} async-done(((bf16[128,4,2048]{0,2,1:T(8,128)(2,1)}), bf16[128,4,2048]{0,2,1:T(8,128)(2,1)S(1)}, u32[]{:S(2)}, u32[]{:S(2)}) %all-to-all-start.1) | async-done | bytes 2097184 | tf_op jit(solution)/shard_map/all_to_all | solution.py:66
  116.6 2.1 copy-done.3
  118.7 4.4 %fusion.24 = (f32[16,128,128]{2,1,0:T(8,128)}, f32[4,16,128,128]{3,2,1,0:T(8,128)}) fusion(bf16[4,128,16,128]{3,1,2,0:T(8,128)(2,1)S(1)} %copy-done.3, f32[4,128,16,128]{1,3,2,0:T(8,128)S(1)} %bitcast.59), kind=kOutput, calls=%fused_computation.39 | convolution fusion | flops 274464768 | bytes 11534336 | tf_op jit(solution)/shard_map/bhtd,bhte->bhde/dot_general | solution.py:76
  123.1 2.4 copy.12
  125.5 3.6 %all-to-all-start = ((bf16[128,4,2048]{0,2,1:T(8,128)(2,1)}), bf16[128,4,2048]{0,2,1:T(8,128)(2,1)S(1)}, u32[]{:S(2)}, u32[]{:S(2)}) async-start(bf16[128,4,2048]{0,2,1:T(8,128)(2,1)} %bitcast.52), calls=%async_computation | async-start | bytes 4194304 | tf_op jit(solution)/shard_map/all_to_all | solution.py:65
  129.2 3.1 %fusion.25 = f32[4,16,128,128]{3,2,1,0:T(8,128)S(1)} fusion(f32[4,16,128,128]{3,2,1,0:T(8,128)} %get-tuple-element.41), kind=kOutput, calls=%fused_computation.40 | output fusion | flops 3145728 | bytes 8388608 | tf_op jit(solution)/shard_map/jit(cumsum)/reduce_window_sum | solution.py:83
  132.4 2.0 slice.20
  134.3 42.5 %all-to-all-done = bf16[128,4,2048]{0,2,1:T(8,128)(2,1)S(1)} async-done(((bf16[128,4,2048]{0,2,1:T(8,128)(2,1)}), bf16[128,4,2048]{0,2,1:T(8,128)(2,1)S(1)}, u32[]{:S(2)}, u32[]{:S(2)}) %all-to-all-start) | async-done | bytes 2097184 | tf_op jit(solution)/shard_map/all_to_all | solution.py:65
  176.8 2.2 convert_element_type.63
  179.0 9.3 %fusion.7 = f32[4,16,128,128]{3,2,1,0:T(8,128)} fusion(bf16[4,128,16,128]{3,1,2,0:T(8,128)(2,1)} %copy.17, pred[128,128]{1,0:T(8,128)(4,1)S(1)} %iota_compare_fusion, f32[4,128,16,128]{1,3,2,0:T(8,128)} %bitcast.61, f32[4,128,16,128]{1,3,2,0:T(8,128)} %bitcast.60), kind=kOutput, calls=%fused_computation.18 | convolution fusion | flops 549453824 | bytes 14696448 | tf_op jit(solution)/shard_map/...hts,...hsd->...htd/dot_general | solution.py:39
  188.4 3.2 %while.10 = (s32[]{:T(128)}, f32[16,128,128]{2,1,0:T(8,128)S(1)}, s32[]{:T(128)}, f32[4,16,128,128]{3,2,1,0:T(8,128)}, s32[]{:T(128)}, /*index=5*/s32[]{:T(128)}, s32[]{:T(128)}) while((s32[]{:T(128)}, f32[16,128,128]{2,1,0:T(8,128)S(1)}, s32[]{:T(128)}, f32[4,16,128,128]{3,2,1,0:T(8,128)}, s32[]{:T(128)}, /*index=5*/s32[]{:T(128)}, ...), condition=%wide.region_2.3_spmd, body=%wide.region_1.2_spmd.sunk | while | flops 262149 | bytes 3145843 | solution.py:29
  188.4 1.5 bitcast_add_fusion.2
  190.0 1.5 bitcast_add_fusion.2
  191.6 5.9 %fusion.18 = bf16[4,128,16,128]{3,1,2,0:T(8,128)(2,1)S(1)} fusion(f32[4,16,128,128]{3,2,1,0:T(8,128)} %fusion.7, f32[3,16,128,128]{3,2,1,0:T(8,128)} %slice.20, f32[16,128,128]{2,1,0:T(8,128)S(1)} %get-tuple-element.28, f32[4,128,16,128]{1,3,2,0:T(8,128)} %bitcast.62), kind=kOutput, calls=%fused_computation.25 | convolution fusion | flops 277872640 | bytes 14680064 | tf_op jit(solution)/shard_map/...htd,...hde->...hte/dot_general | solution.py:42
  199.5 2.2 fusion.3
  204.9 13.8 %collective-permute-done = bf16[128,2048]{1,0:T(8,128)(2,1)S(1)} collective-permute-done((bf16[128,2048]{1,0:T(8,128)(2,1)}, bf16[128,2048]{1,0:T(8,128)(2,1)S(1)}, u32[]{:S(2)}, u32[]{:S(2)}) %collective-permute-start) | collective-permute-done | bytes 524320 | tf_op jit(solution)/shard_map/ppermute | solution.py:16
  218.8 30.3 %collective-permute-done.1 = bf16[128,2048]{1,0:T(8,128)(2,1)S(1)} collective-permute-done((bf16[128,2048]{1,0:T(8,128)(2,1)}, bf16[128,2048]{1,0:T(8,128)(2,1)S(1)}, u32[]{:S(2)}, u32[]{:S(2)}) %collective-permute-start.1) | collective-permute-done | bytes 524320 | tf_op jit(solution)/shard_map/ppermute | solution.py:16
  252.0 1.9 fusion.4
  (32 shorter events, 9.8 us)
Async XLA Ops:
  10.6 53.1 %all-to-all-start.2 = ((bf16[128,4,2048]{0,2,1:T(8,128)(2,1)}), bf16[128,4,2048]{0,2,1:T(8,128)(2,1)S(1)}, u32[]{:S(2)}, u32[]{:S(2)}) async-start(bf16[128,4,2048]{0,2,1:T(8,128)(2,1)} %bitcast.55), calls=%async_computation.2 | async-start | bytes 4194304 | tf_op jit(solution)/shard_map/all_to_all | solution.py:67
  63.7 1.3 copy-start
  65.0 51.3 %all-to-all-start.1 = ((bf16[128,4,2048]{0,2,1:T(8,128)(2,1)}), bf16[128,4,2048]{0,2,1:T(8,128)(2,1)S(1)}, u32[]{:S(2)}, u32[]{:S(2)}) async-start(bf16[128,4,2048]{0,2,1:T(8,128)(2,1)} %bitcast.54), calls=%async_computation.1 | async-start | bytes 4194304 | tf_op jit(solution)/shard_map/all_to_all | solution.py:66
  68.6 119.7 %all-gather.3.cloned.1.call-start = ((), (), s32[]{:S(2)}) async-start(), calls=%async_computation.3 | async-start | bytes 5242880 | tf_op jit(solution)/shard_map/all_gather | solution.py:23
  116.3 2.4 copy-start.3
  116.5 6.5 %copy-start.1 = (f32[128,4,2048]{0,2,1:T(8,128)}, f32[128,4,2048]{0,2,1:T(8,128)S(1)}, u32[]{:S(2)}) copy-start(f32[128,4,2048]{0,2,1:T(8,128)S(1)} %convert_element_type.64) | copy-start | bytes 12582916
  118.7 4.4 %copy-start.2 = (bf16[1,128,8192]{2,1,0:T(8,128)(2,1)S(1)}, bf16[1,128,8192]{2,1,0:T(8,128)(2,1)}, u32[]{:S(2)}) copy-start(bf16[1,128,8192]{2,1,0:T(8,128)(2,1)} %param.6) | copy-start | bytes 6291460
  125.5 51.3 %all-to-all-start = ((bf16[128,4,2048]{0,2,1:T(8,128)(2,1)}), bf16[128,4,2048]{0,2,1:T(8,128)(2,1)S(1)}, u32[]{:S(2)}, u32[]{:S(2)}) async-start(bf16[128,4,2048]{0,2,1:T(8,128)(2,1)} %bitcast.52), calls=%async_computation | async-start | bytes 4194304 | tf_op jit(solution)/shard_map/all_to_all | solution.py:65
  202.8 15.9 %collective-permute-start = (bf16[128,2048]{1,0:T(8,128)(2,1)}, bf16[128,2048]{1,0:T(8,128)(2,1)S(1)}, u32[]{:S(2)}, u32[]{:S(2)}) collective-permute-start(bf16[128,2048]{1,0:T(8,128)(2,1)} %get-tuple-element.39), channel_id=1, source_target_pairs={{0,12},{4,0},{8,4},{12,8},{1,13},{5,1},{9,5},{13,9},{2,14},{6,2},{... | collective-permute-start | bytes 1572872 | tf_op jit(solution)/shard_map/ppermute | solution.py:16
  204.3 44.8 %collective-permute-start.1 = (bf16[128,2048]{1,0:T(8,128)(2,1)}, bf16[128,2048]{1,0:T(8,128)(2,1)S(1)}, u32[]{:S(2)}, u32[]{:S(2)}) collective-permute-start(bf16[128,2048]{1,0:T(8,128)(2,1)} %get-tuple-element.38), channel_id=1, source_target_pairs={{0,8},{4,12},{8,0},{12,4},{1,9},{5,13},{9,1},{13,5},{2,10},{6,14},... | collective-permute-start | bytes 1572872 | tf_op jit(solution)/shard_map/ppermute | solution.py:16
  204.3 44.8 %collective-permute-start.2 = (bf16[128,2048]{1,0:T(8,128)(2,1)}, bf16[128,2048]{1,0:T(8,128)(2,1)}, u32[]{:S(2)}, u32[]{:S(2)}) collective-permute-start(bf16[128,2048]{1,0:T(8,128)(2,1)} %get-tuple-element.37), channel_id=1, source_target_pairs={{0,4},{4,8},{8,12},{12,0},{1,5},{5,9},{9,13},{13,1},{2,6},{6,10},{... | collective-permute-start | bytes 1572872 | tf_op jit(solution)/shard_map/ppermute | solution.py:16
  249.1 2.9 %copy-start.4 = (f32[8192]{0:T(1024)S(1)}, f32[8192]{0:T(1024)}, u32[]{:S(2)}) copy-start(f32[8192]{0:T(1024)} %param.9) | copy-start | bytes 98308
Sparse Core Ops, SparseCore 0:
  123.2 32.4 all-gather.2
